TPU v7x, 32 devices: a whole 2x2x4 slice. The times are simulated.
32 devices in a mesh: fsdp: 4 (over x, core), ctx: 2 (over y), tp: 4 (over z).
Axes of the slice: x: 2, y: 2, z: 4, core: 2. Of those that a mesh axis runs over, the one named last changes fastest.
Arguments:
- tokens: bfloat16 [8, 1024, 2048], P('fsdp', 'ctx'), may hold values from -6 to 6
- attn_gain: bfloat16 [2048], P('fsdp'), may hold values from 0.5 to 1.5
- w_query: bfloat16 [2048, 1024], P('fsdp', 'tp'), may hold values from -0.125 to 0.125
- key_matrix: bfloat16 [2048, 256], P('fsdp', 'tp'), may hold values from -0.125 to 0.125
- value_matrix: bfloat16 [2048, 256], P('fsdp', 'tp'), may hold values from -0.125 to 0.125
- query_gain: bfloat16 [64], P('fsdp'), may hold values from 0.5 to 1.5
- key_gain: bfloat16 [64], P('fsdp'), may hold values from 0.5 to 1.5
- w_out: bfloat16 [1024, 2048], P('tp', 'fsdp'), may hold values from -6 to 6
- ffn_gain: bfloat16 [2048], P('fsdp'), may hold values from 0.5 to 1.5
- w_gate: bfloat16 [2048, 1024], P('fsdp', 'tp'), may hold values from -0.125 to 0.125
- w_up: bfloat16 [2048, 1024], P('fsdp', 'tp'), may hold values from -0.125 to 0.125
- w_down: bfloat16 [1024, 2048], P('tp', 'fsdp'), may hold values from -0.1875 to 0.1875
- prefix_len: int32 [8], P('fsdp'), may hold values from 102 to 512
- out_grad: bfloat16 [8, 1024, 2048], P('fsdp', 'ctx'), may hold values from -6 to 6
Outputs:
- layer_out: bfloat16 [8, 1024, 2048], P('fsdp', 'ctx')
- input_grad: bfloat16 [8, 1024, 2048], P('fsdp', 'ctx')
- grad_attn_gain: float32 [2048], P('fsdp')
- grad_query: float32 [2048, 1024], P('fsdp', 'tp')
- grad_key: float32 [2048, 256], P('fsdp', 'tp')
- grad_value: float32 [2048, 256], P('fsdp', 'tp')
- grad_query_gain: float32 [64], P('fsdp')
- grad_key_gain: float32 [64], P('fsdp')
- grad_out: float32 [1024, 2048], P('tp', 'fsdp')
- grad_ffn_gain: float32 [2048], P('fsdp')
- grad_gate: float32 [2048, 1024], P('fsdp', 'tp')
- grad_up: float32 [2048, 1024], P('fsdp', 'tp')
- grad_down: float32 [1024, 2048], P('tp', 'fsdp')
All inputs are finite; a program needn't handle non-finite values.
Results may differ from a plain program's by a relative error of at most 0.025.
Values may be sent and summed in bfloat16 or wider, within the bound.
No kernel may reach another device: no remote copies, remote signals or barrier semaphores. Data moves between devices by JAX's collectives and lax.ppermute only.
A program may use at most 192 MiB of HBM per device.

v0:
```python
import functools
import jax
import jax.numpy as jnp
from jax import lax
from jax.sharding import PartitionSpec as P

EPSILON = 1e-06
NEGATIVE = -1e30
ROPE_BASE = 10000.0


def rms_norm(values, gain):
    return values * lax.rsqrt(jnp.mean(values * values, axis=-1, keepdims=True) + EPSILON) * gain


def rotate(values, cos_table, sin_table):
    half_dim = values.shape[-1] // 2
    turned = jnp.concatenate([-values[..., half_dim:], values[..., :half_dim]], axis=-1)
    return values * cos_table + turned * sin_table


def rotary_tables(positions, head_dim):
    inverse_freq = ROPE_BASE ** (-jnp.arange(0, head_dim, 2).astype(jnp.float32) / head_dim)
    angles = positions.astype(jnp.float32)[:, None] * inverse_freq[None, :]
    cos_half = jnp.cos(angles)
    sin_half = jnp.sin(angles)
    return (jnp.concatenate([cos_half, cos_half], -1), jnp.concatenate([sin_half, sin_half], -1))


def query_key_post(
    query_raw, unnormed_key, query_gain, key_gain, cos_table, sin_table, seq_count, block_len
):
    head_dim = query_gain.shape[0]
    query_heads = query_raw.reshape(seq_count, block_len, -1, head_dim)
    key_heads = unnormed_key.reshape(seq_count, block_len, -1, head_dim)
    cos_wide = cos_table[None, :, None, :]
    sin_wide = sin_table[None, :, None, :]
    return (
        rotate(rms_norm(query_heads, query_gain), cos_wide, sin_wide),
        rotate(rms_norm(key_heads, key_gain), cos_wide, sin_wide),
    )


def swiglu(gate_proj, up_proj):
    return jax.nn.silu(gate_proj) * up_proj


def outer_sum(left, right):
    return lax.dot_general(
        left, right, (((0,), (0,)), ((), ())), preferred_element_type=jnp.float32
    )


def times_transposed(left, right):
    return lax.dot_general(
        left, right, (((1,), (1,)), ((), ())), preferred_element_type=jnp.float32
    )


def pack_grads(gradients, grad_dims, pieces):
    columns = [
        jnp.moveaxis(gradient, dim_index, 0).reshape(pieces, -1)
        for gradient, dim_index in zip(gradients, grad_dims)
    ]
    return jnp.concatenate(columns, axis=1)


def unpack_grads(packed, gradients, grad_dims, pieces):
    results = []
    offset = 0
    for gradient, dim_index in zip(gradients, grad_dims):
        moved_shape = jnp.moveaxis(gradient, dim_index, 0).shape
        width = gradient.size // pieces
        segment = packed[:, offset : offset + width]
        offset = offset + width
        shaped = segment.reshape((-1,) + tuple(moved_shape[1:]))
        results.append(jnp.moveaxis(shaped, 0, dim_index))
    return results


def shards(
    tokens,
    attn_gain,
    w_query,
    key_matrix,
    value_matrix,
    query_gain,
    key_gain,
    w_out,
    ffn_gain,
    w_gate,
    w_up,
    w_down,
    prefix_len,
    out_grad,
):
    (
        full_attn_gain,
        full_query,
        full_key,
        full_value,
        full_query_gain,
        full_key_gain,
        full_out,
        full_ffn_gain,
        full_gate,
        full_up,
        full_down,
    ) = (
        lax.all_gather(attn_gain, "fsdp", axis=0, tiled=True),
        lax.all_gather(w_query, "fsdp", axis=0, tiled=True),
        lax.all_gather(key_matrix, "fsdp", axis=0, tiled=True),
        lax.all_gather(value_matrix, "fsdp", axis=0, tiled=True),
        lax.all_gather(query_gain, "fsdp", axis=0, tiled=True),
        lax.all_gather(key_gain, "fsdp", axis=0, tiled=True),
        lax.all_gather(w_out, "fsdp", axis=1, tiled=True),
        lax.all_gather(ffn_gain, "fsdp", axis=0, tiled=True),
        lax.all_gather(w_gate, "fsdp", axis=0, tiled=True),
        lax.all_gather(w_up, "fsdp", axis=0, tiled=True),
        lax.all_gather(w_down, "fsdp", axis=1, tiled=True),
    )
    seq_count, block_len, model_dim = tokens.shape
    token_rows = seq_count * block_len
    head_dim = full_query_gain.shape[0]
    head_count = full_query.shape[1] // head_dim
    kv_count = full_key.shape[1] // head_dim
    group_size = head_count // kv_count
    ctx_count = lax.axis_size("ctx")
    ctx_index = lax.axis_index("ctx")
    fsdp_count = lax.axis_size("fsdp")
    seq_len = block_len * ctx_count
    scale_factor = head_dim ** (-0.5)
    tp_count = lax.axis_size("tp")
    share_rows = token_rows // tp_count
    share_start = lax.axis_index("tp") * share_rows

    def own_rows(values):
        return lax.dynamic_slice_in_dim(values, share_start, share_rows, 0)

    query_pos = ctx_index * block_len + jnp.arange(block_len, dtype=jnp.int32)
    cos_table, sin_table = rotary_tables(query_pos, head_dim)
    attn_gain32 = full_attn_gain.astype(jnp.float32)
    ffn_gain32 = full_ffn_gain.astype(jnp.float32)
    query_gain32 = full_query_gain.astype(jnp.float32)
    key_gain32 = full_key_gain.astype(jnp.float32)
    inputs = tokens.astype(jnp.float32).reshape(token_rows, model_dim)
    normalized_input = rms_norm(inputs, attn_gain32).astype(jnp.bfloat16)
    query_raw = jnp.dot(normalized_input, full_query, preferred_element_type=jnp.float32)
    unnormed_key = jnp.dot(normalized_input, full_key, preferred_element_type=jnp.float32)
    value_reduced = jnp.dot(
        normalized_input, full_value, preferred_element_type=jnp.float32
    ).astype(jnp.bfloat16)
    post_fn = functools.partial(
        query_key_post,
        cos_table=cos_table,
        sin_table=sin_table,
        seq_count=seq_count,
        block_len=block_len,
    )
    (rotated_query, key_rot), post_pull = jax.vjp(
        post_fn, query_raw, unnormed_key, query_gain32, key_gain32
    )
    query_grp = rotated_query.astype(jnp.bfloat16).reshape(
        seq_count, block_len, kv_count, group_size, head_dim
    )
    key_low = key_rot.astype(jnp.bfloat16)
    value_heads = value_reduced.reshape(seq_count, block_len, kv_count, head_dim)
    keys_all, values_all = (
        lax.all_gather(key_low, "ctx", axis=1, tiled=True),
        lax.all_gather(value_heads, "ctx", axis=1, tiled=True),
    )
    key_blocks = jnp.moveaxis(
        keys_all.reshape(seq_count, ctx_count, block_len, kv_count, head_dim), 1, 0
    )
    value_blocks = jnp.moveaxis(
        values_all.reshape(seq_count, ctx_count, block_len, kv_count, head_dim), 1, 0
    )
    block_ids = jnp.arange(ctx_count, dtype=jnp.int32)

    def score_block(key_blk, block_id):
        raw_scores = (
            jnp.einsum("sqkgd,sjkd->skgqj", query_grp, key_blk, preferred_element_type=jnp.float32)
            * scale_factor
        )
        key_pos = block_id * block_len + jnp.arange(block_len, dtype=jnp.int32)
        causal = key_pos[None, :] <= query_pos[:, None]
        opened = key_pos[None, None, :] < prefix_len[:, None, None]
        allowed = causal[None] | opened
        return jnp.where(allowed[:, None, None], raw_scores, NEGATIVE)

    def max_step(run_state, scan_item):
        key_blk, block_id = scan_item
        run_max, run_sum = run_state
        scores = score_block(key_blk, block_id)
        new_max = jnp.maximum(run_max, jnp.max(scores, axis=-1))
        new_sum = run_sum * jnp.exp(run_max - new_max) + jnp.sum(
            jnp.exp(scores - new_max[..., None]), axis=-1
        )
        new_state = (new_max, new_sum)
        return (new_state, None)

    stat_shape = (seq_count, kv_count, group_size, block_len)
    (run_max, run_sum), _ = lax.scan(
        max_step,
        (jnp.full(stat_shape, NEGATIVE, jnp.float32), jnp.zeros(stat_shape, jnp.float32)),
        (key_blocks, block_ids),
    )
    log_total = run_max + jnp.log(run_sum)

    def out_step(running, scan_item):
        key_blk, value_blk, block_id = scan_item
        prob_vals = jnp.exp(score_block(key_blk, block_id) - log_total[..., None])
        new_running = running + jnp.einsum(
            "skgqj,sjkd->sqkgd",
            prob_vals.astype(jnp.bfloat16),
            value_blk,
            preferred_element_type=jnp.float32,
        )
        return (new_running, None)

    out_shape = (seq_count, block_len, kv_count, group_size, head_dim)
    attended, _ = lax.scan(
        out_step, jnp.zeros(out_shape, jnp.float32), (key_blocks, value_blocks, block_ids)
    )
    attended_low = attended.reshape(token_rows, head_count * head_dim).astype(jnp.bfloat16)
    attn_part = jnp.dot(attended_low, full_out, preferred_element_type=jnp.float32)
    residual = inputs + lax.psum(attn_part.astype(jnp.bfloat16), "tp").astype(jnp.float32)
    residual_own = own_rows(residual)
    ffn_in = rms_norm(residual, ffn_gain32).astype(jnp.bfloat16)
    gate_proj = jnp.dot(ffn_in, full_gate, preferred_element_type=jnp.float32)
    up_proj = jnp.dot(ffn_in, full_up, preferred_element_type=jnp.float32)
    hidden_f, swiglu_pull = jax.vjp(swiglu, gate_proj, up_proj)
    hidden = hidden_f.astype(jnp.bfloat16)
    ffn_part = jnp.dot(hidden, full_down, preferred_element_type=jnp.float32)
    layer_low = (
        residual + lax.psum(ffn_part.astype(jnp.bfloat16), "tp").astype(jnp.float32)
    ).astype(jnp.bfloat16)
    grad_low = out_grad.reshape(token_rows, model_dim)
    grad_down = outer_sum(hidden, grad_low)
    dhidden = times_transposed(grad_low, full_down)
    dgate_f, dup_f = swiglu_pull(dhidden)
    dgate = dgate_f.astype(jnp.bfloat16)
    dup = dup_f.astype(jnp.bfloat16)
    grad_gate = outer_sum(ffn_in, dgate)
    grad_up = outer_sum(ffn_in, dup)
    dffn_part = times_transposed(dgate, full_gate) + times_transposed(dup, full_up)
    dffn_in = lax.psum(dffn_part.astype(jnp.bfloat16), "tp").astype(jnp.float32)
    _, ffn_norm_pull = jax.vjp(rms_norm, residual, ffn_gain32)
    dres_norm, _ = ffn_norm_pull(dffn_in)
    dresidual = grad_low.astype(jnp.float32) + dres_norm
    _, own_pull = jax.vjp(rms_norm, residual_own, ffn_gain32)
    _, grad_ffn_gain = own_pull(own_rows(dffn_in))
    dres_low = dresidual.astype(jnp.bfloat16)
    grad_out = outer_sum(attended_low, dres_low)
    dattended = times_transposed(dres_low, full_out).astype(jnp.bfloat16)
    dout_grp = dattended.reshape(out_shape)
    delta = jnp.transpose(jnp.sum(dout_grp.astype(jnp.float32) * attended, axis=-1), (0, 2, 3, 1))

    def back_step(running, scan_item):
        key_blk, value_blk, block_id = scan_item
        prob_vals = jnp.exp(score_block(key_blk, block_id) - log_total[..., None])
        prob_low = prob_vals.astype(jnp.bfloat16)
        value_grad = jnp.einsum(
            "skgqj,sqkgd->sjkd", prob_low, dout_grp, preferred_element_type=jnp.float32
        )
        dprob = jnp.einsum(
            "sqkgd,sjkd->skgqj", dout_grp, value_blk, preferred_element_type=jnp.float32
        )
        dscore = (prob_vals * (dprob - delta[..., None])).astype(jnp.bfloat16)
        new_running = (
            running
            + jnp.einsum("skgqj,sjkd->sqkgd", dscore, key_blk, preferred_element_type=jnp.float32)
            * scale_factor
        )
        key_grad = (
            jnp.einsum("skgqj,sqkgd->sjkd", dscore, query_grp, preferred_element_type=jnp.float32)
            * scale_factor
        )
        return (new_running, (key_grad, value_grad))

    dquery_rot, (key_grads, value_grads) = lax.scan(
        back_step, jnp.zeros(out_shape, jnp.float32), (key_blocks, value_blocks, block_ids)
    )
    key_grads = jnp.moveaxis(key_grads, 0, 1).reshape(seq_count, seq_len, kv_count, head_dim)
    value_grads = jnp.moveaxis(value_grads, 0, 1).reshape(seq_count, seq_len, kv_count, head_dim)
    stacked_grads = jnp.stack((key_grads, value_grads), axis=0)
    owned_grads = lax.psum_scatter(
        stacked_grads.astype(jnp.bfloat16), "ctx", scatter_dimension=2, tiled=True
    ).astype(jnp.float32)
    dkey_rot = owned_grads[0]
    dvalue = owned_grads[1]
    dquery_raw, dkey_raw, grad_query_gain, grad_key_gain = post_pull(
        (dquery_rot.reshape(seq_count, block_len, head_count, head_dim), dkey_rot)
    )
    dq_low = dquery_raw.astype(jnp.bfloat16)
    dk_low = dkey_raw.astype(jnp.bfloat16)
    dv_low = dvalue.reshape(token_rows, kv_count * head_dim).astype(jnp.bfloat16)
    grad_query = outer_sum(normalized_input, dq_low)
    grad_key = outer_sum(normalized_input, dk_low)
    grad_value = outer_sum(normalized_input, dv_low)
    dnormed_part = (
        times_transposed(dq_low, full_query)
        + times_transposed(dk_low, full_key)
        + times_transposed(dv_low, full_value)
    )
    dnormed, grad_query_gain, grad_key_gain, grad_ffn_gain = (
        lax.psum(dnormed_part.astype(jnp.bfloat16), "tp").astype(jnp.float32),
        lax.psum(grad_query_gain.astype(jnp.bfloat16), "tp").astype(jnp.float32),
        lax.psum(grad_key_gain.astype(jnp.bfloat16), "tp").astype(jnp.float32),
        lax.psum(grad_ffn_gain.astype(jnp.bfloat16), "tp").astype(jnp.float32),
    )
    _, attn_norm_pull = jax.vjp(rms_norm, inputs, attn_gain32)
    dinput_norm, grad_attn_gain = attn_norm_pull(dnormed)
    input_grad = (dresidual + dinput_norm).astype(jnp.bfloat16)
    gradients = (
        grad_attn_gain,
        grad_query,
        grad_key,
        grad_value,
        grad_query_gain,
        grad_key_gain,
        grad_out,
        grad_ffn_gain,
        grad_gate,
        grad_up,
        grad_down,
    )
    grad_dims = (0, 0, 0, 0, 0, 0, 1, 0, 0, 0, 1)
    piece_count = fsdp_count * ctx_count
    packed = pack_grads(gradients, grad_dims, piece_count)
    reduced = lax.psum_scatter(
        packed.astype(jnp.bfloat16), ("fsdp", "ctx"), scatter_dimension=0, tiled=True
    ).astype(jnp.float32)
    collected_rows = lax.all_gather(reduced.astype(jnp.bfloat16), "ctx", axis=0, tiled=True).astype(
        reduced.dtype
    )
    collected = unpack_grads(collected_rows, gradients, grad_dims, piece_count)
    return (
        layer_low.reshape(seq_count, block_len, model_dim),
        input_grad.reshape(seq_count, block_len, model_dim),
        collected[0],
        collected[1],
        collected[2],
        collected[3],
        collected[4],
        collected[5],
        collected[6],
        collected[7],
        collected[8],
        collected[9],
        collected[10],
    )


def solution(mesh):
    placed = (
        P("fsdp", "ctx", None),
        P("fsdp"),
        P("fsdp", "tp"),
        P("fsdp", "tp"),
        P("fsdp", "tp"),
        P("fsdp"),
        P("fsdp"),
        P("tp", "fsdp"),
        P("fsdp"),
        P("fsdp", "tp"),
        P("fsdp", "tp"),
        P("tp", "fsdp"),
        P("fsdp"),
        P("fsdp", "ctx", None),
    )
    return jax.shard_map(
        shards,
        mesh=mesh,
        in_specs=placed,
        out_specs=(
            P("fsdp", "ctx", None),
            P("fsdp", "ctx", None),
            P("fsdp"),
            P("fsdp", "tp"),
            P("fsdp", "tp"),
            P("fsdp", "tp"),
            P("fsdp"),
            P("fsdp"),
            P("tp", "fsdp"),
            P("fsdp"),
            P("fsdp", "tp"),
            P("fsdp", "tp"),
            P("tp", "fsdp"),
        ),
        check_vma=False,
    )
```

profile of v0, /device:TPU:0, one launch (start us, length us, event | category | flops | bytes accessed | tf_op | source)
XLA Modules:
  0.0 1090.8 jit_solution(5404489563238779598)
XLA Ops:
  12.7 6.2 all-gather
  18.9 8.2 all_gather.45
  34.2 7.3 all-reduce.9
  42.2 5.6 all_gather.47
  48.1 5.4 fusion.87
  53.5 5.8 all_gather.43
  60.8 6.9 all_gather.44
  75.6 22.4 %while.39 = (s32[]{:T(128)}, f32[2,1,4,512]{3,2,0,1:T(4,128)S(1)}, f32[2,1,4,512]{3,2,0,1:T(4,128)S(1)}, s32[2]{0:T(128)S(1)}, s32[2]{0:T(128)S(1)}, /*index=5*/...) while((s32[]{:T(128)}, f32[2,1,4,512]{3,2,0,1:T(4,128)S(1)}, ...), condition=%wide.region_6.7_spmd.clone, body=%wide.region_3.6_spmd.clone.sunk | while | flops 283924480 | bytes 19755172 | solution.py:203
  77.5 4.9 fusion.189
  82.4 4.4 exponential_reduce_fusion.2
  88.7 4.9 fusion.189
  93.6 4.4 exponential_reduce_fusion.2
  98.7 11.8 %while.40 = (s32[]{:T(128)}, f32[2,512,1,4,64]{1,4,3,0,2:T(8,128)S(1)}, bf16[2,2,512,1,64]{2,4,1,3,0:T(8,128)(2,1)}, s32[2]{0:T(128)S(1)}, s32[2]{0:T(128)S(1)},...) while((s32[]{:T(128)}, ...), condition=%wide.region_8.9_spmd.clone, body=%wide.region_7.8_spmd.clone.sunk | while | flops 546572288 | bytes 4486311 | solution.py:222
  111.2 4.7 convolution_convert_fusion.1
  117.8 5.4 all-gather.1
  123.1 148.3 %all-reduce.15.cloned.1.call-done = bf16[1024,2048]{1,0:T(8,128)(2,1)} async-done(((bf16[1024,2048]{1,0:T(8,128)(2,1)}), bf16[1024,2048]{1,0:T(8,128)(2,1)}) %all-reduce.15.cloned.1.call-update) | async-done | bytes 4194320 | tf_op jit(solution)/shard_map/psum | solution.py:227
  271.4 5.0 multiply_reduce_fusion.1
  277.3 6.0 bitcast_add_fusion.1
  283.3 5.2 all-gather.14.cloned.1.call-done
  288.5 4.8 fusion.122
  293.3 13.3 %all-gather.16.cloned.1.call-done = bf16[2048,256]{1,0:T(8,128)(2,1)} async-done(((bf16[512,256]{1,0:T(8,128)(2,1)}), bf16[2048,256]{1,0:T(8,128)(2,1)}) %all-gather.16.cloned.1.call-update) | async-done | bytes 1048592 | tf_op jit(solution)/shard_map/all_gather | solution.py:119
  306.7 4.7 fusion.123
  311.4 13.4 %all-gather.18.cloned.1.call-done = bf16[256,2048]{1,0:T(8,128)(2,1)} async-done(((bf16[256,512]{1,0:T(8,128)(2,1)}), bf16[256,2048]{1,0:T(8,128)(2,1)}) %all-gather.18.cloned.1.call-update) | async-done | bytes 1048592 | tf_op jit(solution)/shard_map/all_gather | solution.py:120
  324.8 4.8 multiply_convert_fusion.1
  334.8 4.4 convolution_convert_fusion
  339.2 150.7 %all-reduce.17.cloned.1.call-done = bf16[1024,2048]{1,0:T(8,128)(2,1)} async-done(((bf16[1024,2048]{1,0:T(8,128)(2,1)}), bf16[1024,2048]{1,0:T(8,128)(2,1)}) %all-reduce.17.cloned.1.call-update) | async-done | bytes 4194320 | tf_op jit(solution)/shard_map/psum | solution.py:247
  489.9 6.8 multiply_reduce_fusion
  497.0 7.4 fusion.80
  513.0 46.1 %while.41 = (s32[]{:T(128)}, f32[2,512,1,4,64]{1,4,3,0,2:T(8,128)S(1)}, bf16[2,2,512,1,64]{2,4,1,3,0:T(8,128)(2,1)}, bf16[2,2,512,1,64]{2,4,1,3,0:T(8,128)(2,1)}...) while((s32[]{:T(128)}, ...), condition=%wide.region_16.17_spmd.clone, body=%wide.region_15.16_spmd.clone.sunk | while | flops 1364789248 | bytes 100594080 | solution.py:281
  519.5 5.1 fusion.206
  529.5 5.7 fusion.209
  542.4 5.1 fusion.206
  552.4 5.7 fusion.209
  566.9 10.8 reduce-scatter.2.cloned.1.call-done
  596.7 4.4 fusion.90
  616.5 4.7 convolution_convert_fusion.5
  630.4 13.4 %all-reduce.7 = (bf16[8,8]{1,0:T(8,128)(2,1)S(1)}, bf16[8,8]{1,0:T(8,128)(2,1)S(1)}, bf16[8,256]{1,0:T(8,128)(2,1)S(1)}) all-reduce(bf16[8,8]{1,0:T(8,128)(2,1)S(1)} %reshape.780, bf16[8,8]{1,0:T(8,128)(2,1)S(1)} %reshape.781, bf16[8,256]{1,0:T(8,128)(2,1)S(1)} %reshape.783), channel_id=1, replica_groups=mesh['fsdp'=4,'ctx'=2,'tp'=4] {'tp'}, use_global_device_ids=true, to_apply=%region_24.25 | all-reduce | flops 2176 | bytes 8704 | tf_op jit(solution)/shard_map/psum | solution.py:308
  643.8 233.6 %all-reduce.21.cloned.1.call-done = (bf16[1024,2048]{1,0:T(8,128)(2,1)}, bf16[1024,2048]{1,0:T(8,128)(2,1)}) async-done(((bf16[1024,2048]{1,0:T(8,128)(2,1)}, bf16[1024,2048]{1,0:T(8,128)(2,1)}), (bf16[1024,2048]{1,0:T(8,128)(2,1)}, bf16[1024,2048]{1,0:T(8,128)(2,1)})) %all-reduce.21.cloned.1.call-update) | async-done | bytes 8388624 | tf_op jit(solution)/shard_map/psum | solution.py:236
  877.5 5.9 fusion.79
  890.5 7.1 dynamic-update-slice.8
  899.0 6.8 dynamic-update-slice.10
  905.8 6.8 dynamic-update-slice.11
  912.6 6.7 dynamic-update-slice.12
  920.1 97.4 %all-reduce.19.cloned.1.call-done = bf16[8,360976]{1,0:T(8,128)(2,1)} async-done(((bf16[8,360976]{1,0:T(8,128)(2,1)}), bf16[8,360976]{1,0:T(8,128)(2,1)}) %all-reduce.19.cloned.1.call-update) | async-done | bytes 5775632
  1017.4 6.1 dynamic-slice_bitcast_fusion
  1023.6 14.9 %fusion.82 = (bf16[1024,2048]{1,0:T(8,128)(2,1)}, bf16[1024,2048]{1,0:T(8,128)(2,1)}) fusion(f32[1024,2048]{1,0:T(8,128)} %copy-done.4, bf16[1024,2048]{1,0:T(8,128)(2,1)} %get-tuple-element.498, bf16[2,512,2048]{2,1,0:T(8,128)(2,1)} %param.20, f32[1024]{0:T(1024)S(1)} %multiply_multiply_fusion.3, f32[2048]{0:T(1024)S(1)} %bitcast.468, ...), kind=kLoop, calls=%fused_computation.93 | loop fusion | flops 29360128 | bytes 33570816 | tf_op jit(solution)/shard_map/convert_element_type | solution.py:314
  1038.5 27.2 %all-gather.20.cloned.1.call-done = bf16[2,1,360976]{2,1,0:T(2,128)(2,1)} async-done(((bf16[1,1,360976]{2,1,0:T(2,128)(2,1)}), bf16[2,1,360976]{2,1,0:T(2,128)(2,1)}) %all-gather.20.cloned.1.call-update) | async-done | bytes 1443920 | tf_op jit(solution)/shard_map/all_gather | solution.py:334
  1065.7 5.0 copy.153
  (354 shorter events, 148.9 us)
Async XLA Ops:
  7.2 61.4 %all-gather.10.cloned.1.call-start = ((), (), s32[]{:S(2)}) async-start(), calls=%async_computation.1 | async-start | bytes 1310720 | tf_op jit(solution)/shard_map/all_gather | solution.py:111
  7.9 103.3 %all-gather.12.cloned.1.call-start = ((), (), s32[]{:S(2)}) async-start(), calls=%async_computation.2 | async-start | bytes 1310720 | tf_op jit(solution)/shard_map/all_gather | solution.py:116
  8.7 262.8 %all-reduce.15.cloned.1.call-start = ((), (), s32[]{:S(2)}) async-start(), calls=%async_computation.3 | async-start | bytes 8388608 | tf_op jit(solution)/shard_map/psum | solution.py:227
  8.8 18.3 %copy-start.1 = (bf16[2,512,2048]{2,1,0:T(8,128)(2,1)S(1)}, bf16[2,512,2048]{2,1,0:T(8,128)(2,1)}, u32[]{:S(2)}) copy-start(bf16[2,512,2048]{2,1,0:T(8,128)(2,1)} %param.20) | copy-start | bytes 12582916
  12.0 19.6 %copy-start.51 = (f32[1,4,2,128]{3,1,2,0:T(4,128)}, f32[1,4,2,128]{3,1,2,0:T(4,128)S(1)}, u32[]{:S(2)}) copy-start(f32[1,4,2,128]{3,1,2,0:T(4,128)S(1)} %copy.136) | copy-start | bytes 12292
  12.0 19.6 %copy-start.49 = (f32[1024]{0:T(1024)}, f32[1024]{0:T(1024)S(1)}, u32[]{:S(2)}) copy-start(f32[1024]{0:T(1024)S(1)} %rsqrt.54) | copy-start | bytes 12292
  18.9 29.2 %copy-start.41 = (f32[4,1,512]{2,1,0:T(1,128)}, f32[4,1,512]{2,1,0:T(1,128)S(1)}, u32[]{:S(2)}) copy-start(f32[4,1,512]{2,1,0:T(1,128)S(1)} %convert_element_type.229) | copy-start | bytes 24580
  27.1 6.6 copy-start.61
  27.1 6.9 copy-start.62
  32.2 21.2 %copy-start.44 = (f32[2,512]{1,0:T(2,128)}, f32[2,512]{1,0:T(2,128)S(1)}, u32[]{:S(2)}) copy-start(f32[2,512]{1,0:T(2,128)S(1)} %rsqrt.55) | copy-start | bytes 12292
  32.5 21.0 %copy-start.12 = (f32[2,512,1,64]{1,0,3,2:T(2,128)}, f32[2,512,1,64]{1,0,3,2:T(2,128)S(1)}, u32[]{:S(2)}) copy-start(f32[2,512,1,64]{1,0,3,2:T(2,128)S(1)} %reshape.768) | copy-start | bytes 786436
  41.6 11.9 %copy-start.55 = (f32[64]{0:T(128)}, f32[64]{0:T(128)S(1)}, u32[]{:S(2)}) copy-start(f32[64]{0:T(128)S(1)} %convert_element_type.189) | copy-start | bytes 772
  41.7 11.8 %copy-start.46 = (bf16[512,64]{0,1:T(8,128)(2,1)S(1)}, bf16[512,64]{0,1:T(8,128)(2,1)}, u32[]{:S(2)}) copy-start(bf16[512,64]{0,1:T(8,128)(2,1)} %param.24) | copy-start | bytes 196612
  42.0 33.0 %copy-start.19 = (f32[512,64]{0,1:T(8,128)}, f32[512,64]{0,1:T(8,128)S(1)}, u32[]{:S(2)}) copy-start(f32[512,64]{0,1:T(8,128)S(1)} %get-tuple-element.546) | copy-start | bytes 393220
  42.1 33.0 %copy-start.21 = (f32[512,64]{0,1:T(8,128)}, f32[512,64]{0,1:T(8,128)S(1)}, u32[]{:S(2)}) copy-start(f32[512,64]{0,1:T(8,128)S(1)} %get-tuple-element.545) | copy-start | bytes 393220
  48.0 11.2 %copy-start.9 = (bf16[1024,2048]{1,0:T(8,128)(2,1)S(1)}, bf16[1024,2048]{1,0:T(8,128)(2,1)}, u32[]{:S(2)}) copy-start(bf16[1024,2048]{1,0:T(8,128)(2,1)} %copy-done.8) | copy-start | bytes 12582916
  53.5 21.6 %copy-start.57 = (f32[64]{0:T(128)}, f32[64]{0:T(128)S(1)}, u32[]{:S(2)}) copy-start(f32[64]{0:T(128)S(1)} %convert_element_type.194) | copy-start | bytes 772
  59.3 15.4 %copy-start.25 = (bf16[2048,64]{0,1:T(8,128)(2,1)}, bf16[2048,64]{0,1:T(8,128)(2,1)S(1)}, u32[]{:S(2)}) copy-start(bf16[2048,64]{0,1:T(8,128)(2,1)S(1)} %all_gather.43) | copy-start | bytes 786436
  111.2 6.5 copy-start.60
  115.9 172.6 %all-gather.14.cloned.1.call-start = ((), (), s32[]{:S(2)}) async-start(), calls=%async_computation.4 | async-start | bytes 1310720 | tf_op jit(solution)/shard_map/all_gather | solution.py:118
  116.5 190.1 %all-gather.16.cloned.1.call-start = ((), (), s32[]{:S(2)}) async-start(), calls=%async_computation.5 | async-start | bytes 1310720 | tf_op jit(solution)/shard_map/all_gather | solution.py:119
  117.1 207.7 %all-gather.18.cloned.1.call-start = ((), (), s32[]{:S(2)}) async-start(), calls=%async_computation.6 | async-start | bytes 1310720 | tf_op jit(solution)/shard_map/all_gather | solution.py:120
  117.7 372.2 %all-reduce.17.cloned.1.call-start = ((), (), s32[]{:S(2)}) async-start(), calls=%async_computation.7 | async-start | bytes 8388608 | tf_op jit(solution)/shard_map/psum | solution.py:247
  334.7 243.0 %reduce-scatter.2.cloned.1.call-start = ((), (), s32[]{:S(2)}) async-start(), calls=%async_computation.8 | async-start | bytes 786432 | tf_op jit(solution)/shard_map/reduce_scatter | solution.py:287
  489.9 6.8 copy-start.3
  489.9 7.1 copy-start.7
  497.0 10.8 copy-start.18
  513.0 46.2 %copy-start.20 = (f32[512,64]{0,1:T(8,128)S(1)}, f32[512,64]{0,1:T(8,128)}, u32[]{:S(2)}) copy-start(f32[512,64]{0,1:T(8,128)} %copy-done.19) | copy-start | bytes 393220
  513.0 6.5 copy-start.36
  535.9 6.5 copy-start.36
  559.1 6.2 copy-start.11
  559.1 6.2 copy-start.22
  559.2 6.2 copy-start.35
  559.2 6.8 copy-start.48
  564.0 313.5 %all-reduce.21.cloned.1.call-start = ((), (), s32[]{:S(2)}) async-start(), calls=%async_computation.11 | async-start | bytes 16777216 | tf_op jit(solution)/shard_map/psum | solution.py:236
  565.3 13.5 %copy-start.13 = (f32[2,512,1,64]{1,0,3,2:T(2,128)S(1)}, f32[2,512,1,64]{1,0,3,2:T(2,128)}, u32[]{:S(2)}) copy-start(f32[2,512,1,64]{1,0,3,2:T(2,128)} %copy-done.12) | copy-start | bytes 786436
  565.3 13.5 %copy-start.45 = (f32[2,512]{1,0:T(2,128)S(1)}, f32[2,512]{1,0:T(2,128)}, u32[]{:S(2)}) copy-start(f32[2,512]{1,0:T(2,128)} %copy-done.44) | copy-start | bytes 12292
  565.3 13.5 %copy-start.56 = (f32[64]{0:T(128)S(1)}, f32[64]{0:T(128)}, u32[]{:S(2)}) copy-start(f32[64]{0:T(128)} %copy-done.55) | copy-start | bytes 772
  565.4 14.2 %copy-start.54 = (f32[2,512]{1,0:T(2,128)S(1)}, f32[2,512]{1,0:T(2,128)}, u32[]{:S(2)}) copy-start(f32[2,512]{1,0:T(2,128)} %copy-done.53) | copy-start | bytes 12292
  565.4 14.5 %copy-start.24 = (bf16[2048,64]{0,1:T(8,128)(2,1)S(1)}, bf16[2048,64]{0,1:T(8,128)(2,1)}, u32[]{:S(2)}) copy-start(bf16[2048,64]{0,1:T(8,128)(2,1)} %copy-done.23) | copy-start | bytes 786436
  586.0 431.4 %all-reduce.19.cloned.1.call-start = ((), (), s32[]{:S(2)}) async-start(), calls=%async_computation.10 | async-start | bytes 11554816
  616.5 6.2 copy-start.59
  622.8 254.7 %copy-start.42 = (f32[4,1,512]{2,1,0:T(1,128)S(1)}, f32[4,1,512]{2,1,0:T(1,128)}, u32[]{:S(2)}) copy-start(f32[4,1,512]{2,1,0:T(1,128)} %copy-done.41) | copy-start | bytes 24580
  622.8 254.7 %copy-start.50 = (f32[1024]{0:T(1024)S(1)}, f32[1024]{0:T(1024)}, u32[]{:S(2)}) copy-start(f32[1024]{0:T(1024)} %copy-done.49) | copy-start | bytes 12292
  883.4 22.5 %copy-start.17 = (bf16[8,65536]{1,0:T(8,128)(2,1)S(1)}, bf16[8,65536]{1,0:T(8,128)(2,1)}, u32[]{:S(2)}) copy-start(bf16[8,65536]{1,0:T(8,128)(2,1)} %reshape.785) | copy-start | bytes 3145732
  899.0 20.4 %copy-start.63 = (u32[32]{0:T(128)S(1)}, u32[32]{0:T(128)}, u32[]{:S(2)}) copy-start(u32[32]{0:T(128)} %constant.133) | copy-start | bytes 388
  912.6 110.9 %copy-start.52 = (f32[1,4,2,128]{3,1,2,0:T(4,128)S(1)}, f32[1,4,2,128]{3,1,2,0:T(4,128)}, u32[]{:S(2)}) copy-start(f32[1,4,2,128]{3,1,2,0:T(4,128)} %copy-done.51) | copy-start | bytes 12292
  919.4 146.3 %all-gather.20.cloned.1.call-start = ((), (), s32[]{:S(2)}) async-start(), calls=%async_computation.9 | async-start | bytes 4333056 | tf_op jit(solution)/shard_map/all_gather | solution.py:334
  (36 other events, 115.1 us)
Sparse Core Ops, SparseCore 0:
  9.5 20.8 all-gather.9
  32.0 16.6 all-gather.11
  116.1 155.3 all-reduce.14
  272.8 15.6 all-gather.13
  289.9 16.6 all-gather.15
  308.1 16.6 all-gather.17
  334.9 154.9 all-reduce.16
  564.1 13.5 reduce-scatter.1
  586.1 291.3 all-reduce.20
  919.5 97.8 all-reduce.18
  1023.7 41.9 all-gather.19
where the time goes:
time: 1100 us; the launch traced here: 1090 us
  waiting for transfers between devices  703 us (64%)
  matrix products  119 us (11%)
  local copies, waits for them, and re-layouts  104 us (9%)
  other arithmetic  84.2 us (8%)
  blocking collectives  58.7 us (5%)
  between operations  16 us (1%)
    psum x1, waiting for transfers between devices, shards(): lax.psum(ffn_part.astype(jnp.bfloat16), 'tp').astype(jnp.float32)  234 us
    psum x1, waiting for transfers between devices, shards(): dffn_in = lax.psum(dffn_part.astype(jnp.bfloat16), 'tp').astype(jnp.float32)  151 us
    psum x1, waiting for transfers between devices, shards(): lax.psum(attn_part.astype(jnp.bfloat16), 'tp').astype(jnp.float32)  148 us
    unnamed x12, waiting for transfers between devices  100 us
    unnamed x152, local copies, waits for them, and re-layouts  57.9 us
    all_gather x1, waiting for transfers between devices, shards(): lax.all_gather(reduced.astype(jnp.bfloat16), 'ctx', axis=0, tiled=True)  27.2 us
    dot_general x7, matrix products, outer_sum(): lax.dot_general(left, right, (((0,), (0,)), ((), ())), preferred_element_...  26.6 us
  transfers between devices with their start and end apart: 11, of which 9 were waited for; matrix products, arithmetic and copies ran while one was open for 13% of the time, Pallas kernels for 0%

commit v1 on v0

--- a/solution.py
+++ b/solution.py
@@ -7,6 +7,12 @@
 EPSILON = 1e-06
 NEGATIVE = -1e30
 ROPE_BASE = 10000.0
+
+
+def add_all(x, name):
+    blocks = lax.all_gather(x, name, axis=0, tiled=False)
+    total = blocks.sum(axis=0)
+    return total
 
 
 def rms_norm(values, gain):
@@ -244,7 +250,7 @@
     grad_gate = outer_sum(ffn_in, dgate)
     grad_up = outer_sum(ffn_in, dup)
     dffn_part = times_transposed(dgate, full_gate) + times_transposed(dup, full_up)
-    dffn_in = lax.psum(dffn_part.astype(jnp.bfloat16), "tp").astype(jnp.float32)
+    dffn_in = add_all(dffn_part.astype(jnp.bfloat16), "tp").astype(jnp.float32)
     _, ffn_norm_pull = jax.vjp(rms_norm, residual, ffn_gain32)
     dres_norm, _ = ffn_norm_pull(dffn_in)
     dresidual = grad_low.astype(jnp.float32) + dres_norm

time: 1100 us -> 1240 us (1.13)
  waiting for transfers between devices: 703 us -> 833 us
    all_gather x0 -> x1, waiting for transfers between devices: none -> 282 us  [add_all(): blocks = lax.all_gather(x, name, axis=0, tiled=False)]
    psum x1 -> x0, waiting for transfers between devices: 151 us -> none  [shards(): dffn_in = lax.psum(dffn_part.astype(jnp.bfloat16), 'tp').astype(jnp.float32)]
  transfers between devices with their start and end apart: 11 -> 11, of which waited for: 9 -> 9; matrix products, arithmetic and copies ran while one was open for 13% -> 12% of each run, Pallas kernels for 0% -> 0%
where the time goes in v1:
time: 1240 us; the launch traced here: 1230 us
  waiting for transfers between devices  833 us (67%)
  matrix products  119 us (10%)
  local copies, waits for them, and re-layouts  105 us (8%)
  other arithmetic  96.2 us (8%)
  blocking collectives  58.1 us (5%)
  between operations  16 us (1%)
    all_gather x1, waiting for transfers between devices, add_all(): blocks = lax.all_gather(x, name, axis=0, tiled=False)  282 us
    psum x1, waiting for transfers between devices, shards(): lax.psum(ffn_part.astype(jnp.bfloat16), 'tp').astype(jnp.float32)  234 us
    psum x1, waiting for transfers between devices, shards(): lax.psum(attn_part.astype(jnp.bfloat16), 'tp').astype(jnp.float32)  148 us
    unnamed x12, waiting for transfers between devices  100 us
    unnamed x152, local copies, waits for them, and re-layouts  57.8 us
    all_gather x1, waiting for transfers between devices, shards(): lax.all_gather(reduced.astype(jnp.bfloat16), 'ctx', axis=0, tiled=True)  27.2 us
    dot_general x7, matrix products, outer_sum(): lax.dot_general(left, right, (((0,), (0,)), ((), ())), preferred_element_...  26.6 us
  transfers between devices with their start and end apart: 11, of which 9 were waited for; matrix products, arithmetic and copies ran while one was open for 12% of the time, Pallas kernels for 0%

profile of v1, /device:TPU:0, one launch (start us, length us, event | category | flops | bytes accessed | tf_op | source)
XLA Modules:
  0.0 1233.2 jit_solution(16332656233213846107)
XLA Ops:
  12.7 6.2 all-gather.1
  18.9 8.2 all_gather.51
  34.2 7.3 all-reduce.9
  42.2 5.6 all_gather.53
  48.1 5.4 fusion.87
  53.5 5.8 all_gather.49
  60.8 6.6 all_gather.50
  75.3 22.4 %while.39 = (s32[]{:T(128)}, f32[2,1,4,512]{3,2,0,1:T(4,128)S(1)}, f32[2,1,4,512]{3,2,0,1:T(4,128)S(1)}, s32[2]{0:T(128)S(1)}, s32[2]{0:T(128)S(1)}, /*index=5*/...) while((s32[]{:T(128)}, f32[2,1,4,512]{3,2,0,1:T(4,128)S(1)}, ...), condition=%wide.region_6.7_spmd.clone, body=%wide.region_3.6_spmd.clone.sunk | while | flops 283924480 | bytes 19755172 | solution.py:209
  77.2 4.9 fusion.189
  82.1 4.4 exponential_reduce_fusion.2
  88.4 4.9 fusion.189
  98.3 11.8 while.40
  110.9 4.7 convolution_convert_fusion.1
  117.4 5.4 all-gather.2
  122.8 148.2 %all-reduce.14.cloned.1.call-done = bf16[1024,2048]{1,0:T(8,128)(2,1)} async-done(((bf16[1024,2048]{1,0:T(8,128)(2,1)}), bf16[1024,2048]{1,0:T(8,128)(2,1)}) %all-reduce.14.cloned.1.call-update) | async-done | bytes 4194320 | tf_op jit(solution)/shard_map/psum | solution.py:233
  271.1 5.0 multiply_reduce_fusion.1
  277.0 6.0 bitcast_add_fusion.1
  283.0 5.2 all-gather.16.cloned.1.call-done
  288.2 4.7 fusion.122
  292.9 13.4 %all-gather.18.cloned.1.call-done = bf16[2048,256]{1,0:T(8,128)(2,1)} async-done(((bf16[512,256]{1,0:T(8,128)(2,1)}), bf16[2048,256]{1,0:T(8,128)(2,1)}) %all-gather.18.cloned.1.call-update) | async-done | bytes 1048592 | tf_op jit(solution)/shard_map/all_gather | solution.py:125
  306.3 4.7 fusion.123
  311.0 13.4 %all-gather.20.cloned.1.call-done = bf16[256,2048]{1,0:T(8,128)(2,1)} async-done(((bf16[256,512]{1,0:T(8,128)(2,1)}), bf16[256,2048]{1,0:T(8,128)(2,1)}) %all-gather.20.cloned.1.call-update) | async-done | bytes 1048592 | tf_op jit(solution)/shard_map/all_gather | solution.py:126
  324.5 4.8 multiply_convert_fusion.1
  334.9 4.4 convolution_convert_fusion
  339.4 282.0 %all-gather.22.cloned.1.call-done = bf16[4096,2048]{1,0:T(8,128)(2,1)} async-done(((bf16[1024,2048]{1,0:T(8,128)(2,1)}), bf16[4096,2048]{1,0:T(8,128)(2,1)}) %all-gather.22.cloned.1.call-update) | async-done | bytes 16777232 | tf_op jit(solution)/shard_map/all_gather | solution.py:13
  621.4 12.2 reduce_sum.161
  633.6 6.8 multiply_reduce_fusion
  640.7 7.2 fusion.80
  656.5 45.8 %while.41 = (s32[]{:T(128)}, f32[2,512,1,4,64]{1,4,3,0,2:T(8,128)S(1)}, bf16[2,2,512,1,64]{2,4,1,3,0:T(8,128)(2,1)}, bf16[2,2,512,1,64]{2,4,1,3,0:T(8,128)(2,1)}...) while((s32[]{:T(128)}, ...), condition=%wide.region_16.17_spmd.clone, body=%wide.region_15.16_spmd.clone.sunk | while | flops 1364789248 | bytes 100594080 | solution.py:287
  663.1 5.1 fusion.206
  673.1 5.7 fusion.209
  685.9 5.1 fusion.206
  695.9 5.7 fusion.209
  710.3 9.8 reduce-scatter.2.cloned.1.call-done
  739.2 4.4 fusion.90
  759.3 4.7 convolution_convert_fusion.5
  773.2 13.1 %all-reduce.7 = (bf16[8,8]{1,0:T(8,128)(2,1)S(1)}, bf16[8,8]{1,0:T(8,128)(2,1)S(1)}, bf16[8,256]{1,0:T(8,128)(2,1)S(1)}) all-reduce(bf16[8,8]{1,0:T(8,128)(2,1)S(1)} %reshape.780, bf16[8,8]{1,0:T(8,128)(2,1)S(1)} %reshape.781, bf16[8,256]{1,0:T(8,128)(2,1)S(1)} %reshape.783), channel_id=1, replica_groups=mesh['fsdp'=4,'ctx'=2,'tp'=4] {'tp'}, use_global_device_ids=true, to_apply=%region_24.25 | all-reduce | flops 2176 | bytes 8704 | tf_op jit(solution)/shard_map/psum | solution.py:314
  786.3 233.7 %all-reduce.18.cloned.1.call-done = (bf16[1024,2048]{1,0:T(8,128)(2,1)}, bf16[1024,2048]{1,0:T(8,128)(2,1)}) async-done(((bf16[1024,2048]{1,0:T(8,128)(2,1)}, bf16[1024,2048]{1,0:T(8,128)(2,1)}), (bf16[1024,2048]{1,0:T(8,128)(2,1)}, bf16[1024,2048]{1,0:T(8,128)(2,1)})) %all-reduce.18.cloned.1.call-update) | async-done | bytes 8388624 | tf_op jit(solution)/shard_map/psum | solution.py:242
  1020.0 5.9 fusion.79
  1032.9 7.1 dynamic-update-slice.8
  1041.5 6.8 dynamic-update-slice.10
  1048.3 6.8 dynamic-update-slice.11
  1055.1 6.8 dynamic-update-slice.12
  1062.5 97.4 %all-reduce.16.cloned.1.call-done = bf16[8,360976]{1,0:T(8,128)(2,1)} async-done(((bf16[8,360976]{1,0:T(8,128)(2,1)}), bf16[8,360976]{1,0:T(8,128)(2,1)}) %all-reduce.16.cloned.1.call-update) | async-done | bytes 5775632
  1159.9 6.1 dynamic-slice_bitcast_fusion
  1166.0 14.9 %fusion.82 = (bf16[1024,2048]{1,0:T(8,128)(2,1)}, bf16[1024,2048]{1,0:T(8,128)(2,1)}) fusion(f32[1024,2048]{1,0:T(8,128)} %copy-done.4, bf16[1024,2048]{1,0:T(8,128)(2,1)} %get-tuple-element.498, bf16[2,512,2048]{2,1,0:T(8,128)(2,1)} %param.20, f32[1024]{0:T(1024)S(1)} %multiply_multiply_fusion.3, f32[2048]{0:T(1024)S(1)} %bitcast.470, ...), kind=kLoop, calls=%fused_computation.93 | loop fusion | flops 29360128 | bytes 33570816 | tf_op jit(solution)/shard_map/convert_element_type | solution.py:320
  1180.9 27.2 %all-gather.24.cloned.1.call-done = bf16[2,1,360976]{2,1,0:T(2,128)(2,1)} async-done(((bf16[1,1,360976]{2,1,0:T(2,128)(2,1)}), bf16[2,1,360976]{2,1,0:T(2,128)(2,1)}) %all-gather.24.cloned.1.call-update) | async-done | bytes 1443920 | tf_op jit(solution)/shard_map/all_gather | solution.py:340
  1208.2 5.0 copy.153
  (355 shorter events, 154.3 us)
Async XLA Ops:
  7.2 61.1 %all-gather.12.cloned.1.call-start = ((), (), s32[]{:S(2)}) async-start(), calls=%async_computation.1 | async-start | bytes 1310720 | tf_op jit(solution)/shard_map/all_gather | solution.py:117
  7.9 102.9 %all-gather.14.cloned.1.call-start = ((), (), s32[]{:S(2)}) async-start(), calls=%async_computation.2 | async-start | bytes 1310720 | tf_op jit(solution)/shard_map/all_gather | solution.py:122
  8.7 262.4 %all-reduce.14.cloned.1.call-start = ((), (), s32[]{:S(2)}) async-start(), calls=%async_computation.3 | async-start | bytes 8388608 | tf_op jit(solution)/shard_map/psum | solution.py:233
  8.8 18.3 %copy-start.1 = (bf16[2,512,2048]{2,1,0:T(8,128)(2,1)S(1)}, bf16[2,512,2048]{2,1,0:T(8,128)(2,1)}, u32[]{:S(2)}) copy-start(bf16[2,512,2048]{2,1,0:T(8,128)(2,1)} %param.20) | copy-start | bytes 12582916
  12.0 19.6 %copy-start.51 = (f32[1,4,2,128]{3,1,2,0:T(4,128)}, f32[1,4,2,128]{3,1,2,0:T(4,128)S(1)}, u32[]{:S(2)}) copy-start(f32[1,4,2,128]{3,1,2,0:T(4,128)S(1)} %copy.136) | copy-start | bytes 12292
  12.0 19.6 %copy-start.49 = (f32[1024]{0:T(1024)}, f32[1024]{0:T(1024)S(1)}, u32[]{:S(2)}) copy-start(f32[1024]{0:T(1024)S(1)} %rsqrt.54) | copy-start | bytes 12292
  18.9 29.2 %copy-start.41 = (f32[4,1,512]{2,1,0:T(1,128)}, f32[4,1,512]{2,1,0:T(1,128)S(1)}, u32[]{:S(2)}) copy-start(f32[4,1,512]{2,1,0:T(1,128)S(1)} %convert_element_type.231) | copy-start | bytes 24580
  27.1 6.6 copy-start.61
  27.1 6.9 copy-start.62
  32.2 21.2 %copy-start.44 = (f32[2,512]{1,0:T(2,128)}, f32[2,512]{1,0:T(2,128)S(1)}, u32[]{:S(2)}) copy-start(f32[2,512]{1,0:T(2,128)S(1)} %rsqrt.55) | copy-start | bytes 12292
  32.5 21.0 %copy-start.12 = (f32[2,512,1,64]{1,0,3,2:T(2,128)}, f32[2,512,1,64]{1,0,3,2:T(2,128)S(1)}, u32[]{:S(2)}) copy-start(f32[2,512,1,64]{1,0,3,2:T(2,128)S(1)} %reshape.768) | copy-start | bytes 786436
  41.6 11.9 copy-start.55
  41.7 11.8 copy-start.46
  42.0 32.7 %copy-start.19 = (f32[512,64]{0,1:T(8,128)}, f32[512,64]{0,1:T(8,128)S(1)}, u32[]{:S(2)}) copy-start(f32[512,64]{0,1:T(8,128)S(1)} %get-tuple-element.546) | copy-start | bytes 393220
  42.1 32.7 %copy-start.21 = (f32[512,64]{0,1:T(8,128)}, f32[512,64]{0,1:T(8,128)S(1)}, u32[]{:S(2)}) copy-start(f32[512,64]{0,1:T(8,128)S(1)} %get-tuple-element.545) | copy-start | bytes 393220
  48.0 11.2 copy-start.9
  53.5 21.3 %copy-start.57 = (f32[64]{0:T(128)}, f32[64]{0:T(128)S(1)}, u32[]{:S(2)}) copy-start(f32[64]{0:T(128)S(1)} %convert_element_type.196) | copy-start | bytes 772
  59.3 15.1 %copy-start.25 = (bf16[2048,64]{0,1:T(8,128)(2,1)}, bf16[2048,64]{0,1:T(8,128)(2,1)S(1)}, u32[]{:S(2)}) copy-start(bf16[2048,64]{0,1:T(8,128)(2,1)S(1)} %all_gather.49) | copy-start | bytes 786436
  110.8 6.5 copy-start.60
  115.6 172.6 %all-gather.16.cloned.1.call-start = ((), (), s32[]{:S(2)}) async-start(), calls=%async_computation.4 | async-start | bytes 1310720 | tf_op jit(solution)/shard_map/all_gather | solution.py:124
  116.2 190.1 %all-gather.18.cloned.1.call-start = ((), (), s32[]{:S(2)}) async-start(), calls=%async_computation.5 | async-start | bytes 1310720 | tf_op jit(solution)/shard_map/all_gather | solution.py:125
  116.8 207.7 %all-gather.20.cloned.1.call-start = ((), (), s32[]{:S(2)}) async-start(), calls=%async_computation.6 | async-start | bytes 1310720 | tf_op jit(solution)/shard_map/all_gather | solution.py:126
  117.3 504.0 %all-gather.22.cloned.1.call-start = ((), (), s32[]{:S(2)}) async-start(), calls=%async_computation.8 | async-start | bytes 20971520 | tf_op jit(solution)/shard_map/all_gather | solution.py:13
  334.4 385.6 %reduce-scatter.2.cloned.1.call-start = ((), (), s32[]{:S(2)}) async-start(), calls=%async_computation.7 | async-start | bytes 786432 | tf_op jit(solution)/shard_map/reduce_scatter | solution.py:293
  633.5 6.8 copy-start.3
  633.5 7.1 copy-start.7
  640.7 10.6 copy-start.18
  656.5 45.9 %copy-start.20 = (f32[512,64]{0,1:T(8,128)S(1)}, f32[512,64]{0,1:T(8,128)}, u32[]{:S(2)}) copy-start(f32[512,64]{0,1:T(8,128)} %copy-done.19) | copy-start | bytes 393220
  656.6 6.5 copy-start.36
  679.5 6.5 copy-start.36
  702.3 6.4 copy-start.11
  702.3 6.4 copy-start.22
  702.3 6.4 copy-start.35
  702.3 6.4 copy-start.58
  702.3 7.0 copy-start.48
  707.1 312.9 %all-reduce.18.cloned.1.call-start = ((), (), s32[]{:S(2)}) async-start(), calls=%async_computation.11 | async-start | bytes 16777216 | tf_op jit(solution)/shard_map/psum | solution.py:242
  708.7 12.5 %copy-start.13 = (f32[2,512,1,64]{1,0,3,2:T(2,128)S(1)}, f32[2,512,1,64]{1,0,3,2:T(2,128)}, u32[]{:S(2)}) copy-start(f32[2,512,1,64]{1,0,3,2:T(2,128)} %copy-done.12) | copy-start | bytes 786436
  708.7 12.5 %copy-start.45 = (f32[2,512]{1,0:T(2,128)S(1)}, f32[2,512]{1,0:T(2,128)}, u32[]{:S(2)}) copy-start(f32[2,512]{1,0:T(2,128)} %copy-done.44) | copy-start | bytes 12292
  708.7 12.5 %copy-start.56 = (f32[64]{0:T(128)S(1)}, f32[64]{0:T(128)}, u32[]{:S(2)}) copy-start(f32[64]{0:T(128)} %copy-done.55) | copy-start | bytes 772
  708.7 13.2 %copy-start.54 = (f32[2,512]{1,0:T(2,128)S(1)}, f32[2,512]{1,0:T(2,128)}, u32[]{:S(2)}) copy-start(f32[2,512]{1,0:T(2,128)} %copy-done.53) | copy-start | bytes 12292
  708.7 13.5 %copy-start.24 = (bf16[2048,64]{0,1:T(8,128)(2,1)S(1)}, bf16[2048,64]{0,1:T(8,128)(2,1)}, u32[]{:S(2)}) copy-start(bf16[2048,64]{0,1:T(8,128)(2,1)} %copy-done.23) | copy-start | bytes 786436
  728.5 431.4 %all-reduce.16.cloned.1.call-start = ((), (), s32[]{:S(2)}) async-start(), calls=%async_computation.10 | async-start | bytes 11554816
  765.6 254.3 %copy-start.42 = (f32[4,1,512]{2,1,0:T(1,128)S(1)}, f32[4,1,512]{2,1,0:T(1,128)}, u32[]{:S(2)}) copy-start(f32[4,1,512]{2,1,0:T(1,128)} %copy-done.41) | copy-start | bytes 24580
  765.6 254.3 %copy-start.50 = (f32[1024]{0:T(1024)S(1)}, f32[1024]{0:T(1024)}, u32[]{:S(2)}) copy-start(f32[1024]{0:T(1024)} %copy-done.49) | copy-start | bytes 12292
  1025.9 22.4 %copy-start.17 = (bf16[8,65536]{1,0:T(8,128)(2,1)S(1)}, bf16[8,65536]{1,0:T(8,128)(2,1)}, u32[]{:S(2)}) copy-start(bf16[8,65536]{1,0:T(8,128)(2,1)} %reshape.785) | copy-start | bytes 3145732
  1041.5 20.5 %copy-start.63 = (u32[32]{0:T(128)S(1)}, u32[32]{0:T(128)}, u32[]{:S(2)}) copy-start(u32[32]{0:T(128)} %constant.135) | copy-start | bytes 388
  1055.1 110.9 %copy-start.52 = (f32[1,4,2,128]{3,1,2,0:T(4,128)S(1)}, f32[1,4,2,128]{3,1,2,0:T(4,128)}, u32[]{:S(2)}) copy-start(f32[1,4,2,128]{3,1,2,0:T(4,128)} %copy-done.51) | copy-start | bytes 12292
  1061.9 146.3 %all-gather.24.cloned.1.call-start = ((), (), s32[]{:S(2)}) async-start(), calls=%async_computation.9 | async-start | bytes 4333056 | tf_op jit(solution)/shard_map/all_gather | solution.py:340
  (36 other events, 115.7 us)
Sparse Core Ops, SparseCore 0:
  9.5 20.8 all-gather.11
  32.0 16.6 all-gather.13
  115.7 155.3 all-reduce.13
  272.5 15.6 all-gather.15
  289.6 16.6 all-gather.17
  307.7 16.6 all-gather.19
  334.6 286.7 all-gather.21
  707.2 12.8 reduce-scatter.1
  728.6 291.3 all-reduce.17
  1062.0 97.8 all-reduce.15
  1166.1 41.9 all-gather.23
